TPU v7x, 32 devices: a whole 2x2x4 slice. The times are simulated.
32 devices in a mesh: groups: 2 (over x), ctx: 16 (over z, y, core).
Axes of the slice: x: 2, y: 2, z: 4, core: 2. Of those that a mesh axis runs over, the one named last changes fastest.
Arguments:
- queries: bfloat16 [4096, 8192], P(('groups', 'ctx')), parts along dimension 0, may hold values from -8 to 8
- new_keys: bfloat16 [4096, 1024], P(('groups', 'ctx')), parts along dimension 0, may hold values from -12 to 12
- new_values: bfloat16 [4096, 1024], P(('groups', 'ctx')), parts along dimension 0, may hold values from -6 to 6
- prefix_keys: bfloat16 [256, 1024], P(('groups', 'ctx')), parts along dimension 0, may hold values from -16 to 16
- prefix_values: bfloat16 [256, 1024], P(('groups', 'ctx')), parts along dimension 0, may hold values from -6 to 6
- pool_keys: bfloat16 [32, 2, 256, 1024], P(('groups', 'ctx')), parts along dimension 0, may hold values from -12 to 12
- pool_values: bfloat16 [32, 2, 256, 1024], P(('groups', 'ctx')), parts along dimension 0, may hold values from -6 to 6
- owners: int32 [4], P('groups'), parts along dimension 0, may hold values from 0 to 15
- lengths: int32 [32], P(('groups', 'ctx')), parts along dimension 0, may hold values from 1 to 128, as said below
Outputs:
- attended: bfloat16 [4096, 8192], P(('groups', 'ctx')), parts along dimension 0
There are 2 independent parts, one for each index of `groups`. A program takes and returns all parts, laid end to end along the dimension named above; each array names one. Nothing has to cross between parts.
Inputs may be any that keep to these rules, and one draw needn't show every extreme that they name: `lengths`: some device's prompt fills all 128 slots.
All inputs are finite; a program needn't handle non-finite values.
Results may differ from a plain program's by a relative error of at most 0.0035.
Values may be sent and summed in bfloat16 or wider, within the bound.
A program may use at most 128 MiB of HBM per device.

v0:
```python
import jax
import jax.numpy as jnp
from jax import lax
from jax.sharding import PartitionSpec as P

H = 64
KVH = 8
HD = 128
SB = 2
BLK = 256


def attend(carried, head_queries, key_rows, value_rows, visible):
    maxima, totals, accums = carried
    new_maxima = []
    new_totals = []
    new_accums = []
    score_scale = 1.0 / HD**0.5
    for kv_head in range(KVH):
        head_keys = key_rows[:, kv_head * HD : (kv_head + 1) * HD]
        head_values = value_rows[:, kv_head * HD : (kv_head + 1) * HD]
        scores = (
            lax.dot_general(
                head_queries[kv_head],
                head_keys,
                (((1,), (1,)), ((), ())),
                preferred_element_type=jnp.float32,
            )
            * score_scale
        )
        if visible is not None:
            scores = jnp.where(visible, scores, -1e30)
        new_max = jnp.maximum(maxima[kv_head], jnp.max(scores, axis=1))
        weights = jnp.exp(scores - new_max[:, None])
        if visible is not None:
            weights = jnp.where(visible, weights, 0.0)
        shrink = jnp.exp(maxima[kv_head] - new_max)
        new_totals.append(totals[kv_head] * shrink + jnp.sum(weights, axis=1))
        summed = jnp.dot(
            weights.astype(jnp.bfloat16), head_values, preferred_element_type=jnp.float32
        )
        new_accums.append(accums[kv_head] * shrink[:, None] + summed)
        new_maxima.append(new_max)
    return (jnp.stack(new_maxima), jnp.stack(new_totals), jnp.stack(new_accums))


def body(
    queries,
    new_keys,
    new_values,
    prefix_keys,
    prefix_values,
    pool_keys,
    pool_values,
    owners,
    lengths,
):
    group_size = H // KVH
    rows_here = queries.shape[0]
    head_queries = [
        queries[:, kv_head * group_size * HD : (kv_head + 1) * group_size * HD].reshape(
            rows_here * group_size, HD
        )
        for kv_head in range(KVH)
    ]
    carried = (
        jnp.full((KVH, rows_here * group_size), -1e30, jnp.float32),
        jnp.zeros((KVH, rows_here * group_size), jnp.float32),
        jnp.zeros((KVH, rows_here * group_size, HD), jnp.float32),
    )
    length = lengths[0]
    positions = jnp.arange(rows_here)
    own_visible = (positions[None, :] <= positions[:, None]) & (positions[None, :] < length)
    own_visible = jnp.repeat(own_visible, group_size, axis=0)
    carried = attend(carried, head_queries, new_keys, new_values, own_visible)
    pages_keys = pool_keys[0]
    pages_values = pool_values[0]
    my_rank = lax.axis_index("ctx")
    owned = (owners == my_rank)[:, None, None]
    mine_keys = jnp.where(owned, pages_keys.astype(jnp.float32), 0.0).reshape(SB * BLK, KVH * HD)
    mine_values = jnp.where(owned, pages_values.astype(jnp.float32), 0.0).reshape(
        SB * BLK, KVH * HD
    )
    part_keys, part_values = (
        lax.psum_scatter(mine_keys, "ctx", scatter_dimension=0, tiled=True),
        lax.psum_scatter(mine_values, "ctx", scatter_dimension=0, tiled=True),
    )
    shared_keys, shared_values = (
        lax.all_gather(part_keys.astype(jnp.bfloat16), "ctx", axis=0, tiled=True),
        lax.all_gather(part_values.astype(jnp.bfloat16), "ctx", axis=0, tiled=True),
    )
    carried = attend(carried, head_queries, shared_keys, shared_values, None)
    whole_keys, whole_values = (
        lax.all_gather(prefix_keys, "ctx", axis=0, tiled=True),
        lax.all_gather(prefix_values, "ctx", axis=0, tiled=True),
    )
    carried = attend(carried, head_queries, whole_keys, whole_values, None)
    maxima, totals, accums = carried
    pieces = [
        (accums[kv_head] / totals[kv_head][:, None]).reshape(rows_here, group_size * HD)
        for kv_head in range(KVH)
    ]
    joined = jnp.concatenate(pieces, axis=1)
    live = positions < length
    return jnp.where(live[:, None], joined, 0.0).astype(jnp.bfloat16)


def solution(mesh):
    placed = (
        P(("groups", "ctx"), None),
        P(("groups", "ctx"), None),
        P(("groups", "ctx"), None),
        P(("groups", "ctx"), None),
        P(("groups", "ctx"), None),
        P(("groups", "ctx"), None, None, None),
        P(("groups", "ctx"), None, None, None),
        P("groups"),
        P(("groups", "ctx")),
    )
    return jax.shard_map(
        body, mesh=mesh, in_specs=placed, out_specs=P(("groups", "ctx"), None), check_vma=False
    )
```

profile of v0, /device:TPU:0, one launch (start us, length us, event | category | flops | bytes accessed | tf_op | source)
XLA Modules:
  0.0 285.9 jit_solution(6476662964461193253)
XLA Ops:
  7.3 3.9 %convert_select_fusion = (f32[512,1024]{1,0:T(8,128)}, f32[512,1024]{1,0:T(8,128)}) fusion(bf16[1,2,256,1024]{3,2,1,0:T(8,128)(2,1)} %param.15, pred[512]{0:T(512)(128)(4,1)S(1)} %broadcast_in_dim.53, bf16[1,2,256,1024]{3,2,1,0:T(8,128)(2,1)} %param.14), kind=kLoop, calls=%fused_computation.1 | loop fusion | flops 2097152 | bytes 6291968 | tf_op jit(solution)/shard_map/jit(_where)/select_n | solution.py:81
  15.4 23.8 %all_gather.14 = bf16[128,1024]{1,0:T(8,128)(2,1)S(1)} all-gather(bf16[8,1024]{1,0:T(8,128)(2,1)S(1)} %copy-done.97), channel_id=1, replica_groups=mesh['groups'=2,'ctx'=16] {'ctx'}, dimensions={0}, use_global_device_ids=true | all-gather | bytes 278528 | tf_op jit(solution)/shard_map/all_gather | solution.py:94
  40.3 1.6 fusion.260
  43.2 1.6 fusion.258
  45.7 1.6 fusion.270
  47.3 1.6 fusion.271
  48.9 27.0 %reduce-scatter.3.cloned.1.call-done = f32[32,1024]{1,0:T(8,128)} async-done(((f32[512,1024]{1,0:T(8,128)}), f32[32,1024]{1,0:T(8,128)}) %reduce-scatter.3.cloned.1.call-update) | async-done | bytes 131088 | tf_op jit(solution)/shard_map/reduce_scatter | solution.py:85
  77.5 21.8 %all_gather.15 = bf16[128,1024]{1,0:T(8,128)(2,1)} all-gather(bf16[8,1024]{1,0:T(8,128)(2,1)} %param.13), channel_id=1, replica_groups=mesh['groups'=2,'ctx'=16] {'ctx'}, dimensions={0}, use_global_device_ids=true | all-gather | bytes 278528 | tf_op jit(solution)/shard_map/all_gather | solution.py:95
  99.9 1.6 fusion.268
  101.5 1.6 fusion.269
  103.1 1.6 fusion.266
  104.8 1.6 fusion.267
  106.4 1.6 fusion.264
  108.0 1.6 fusion.265
  109.7 1.6 fusion.272
  111.3 1.6 fusion.273
  112.9 27.5 %reduce-scatter.5.cloned.1.call-done = f32[32,1024]{1,0:T(8,128)} async-done(((f32[512,1024]{1,0:T(8,128)}), f32[32,1024]{1,0:T(8,128)}) %reduce-scatter.5.cloned.1.call-update) | async-done | bytes 131088 | tf_op jit(solution)/shard_map/reduce_scatter | solution.py:86
  142.0 37.4 %all-gather.3.cloned.1.call-done = bf16[512,1024]{1,0:T(8,128)(2,1)} async-done(((bf16[32,1024]{1,0:T(8,128)(2,1)}), bf16[512,1024]{1,0:T(8,128)(2,1)}) %all-gather.3.cloned.1.call-update) | async-done | bytes 1048592 | tf_op jit(solution)/shard_map/all_gather | solution.py:89
  179.4 1.5 multiply_reduce_fusion
  182.3 1.7 fusion.94
  184.0 2.1 fusion.120
  186.2 2.8 multiply_reduce_fusion.1
  191.3 1.7 multiply_reduce_fusion.2
  194.4 1.8 multiply_reduce_fusion.3
  197.5 1.8 multiply_reduce_fusion.4
  200.6 1.8 multiply_reduce_fusion.5
  204.8 1.8 multiply_reduce_fusion.7
  215.6 2.0 fusion.41
  218.2 3.3 %fusion.54 = bf16[1024,128]{1,0:T(8,128)(2,1)} fusion(f32[1024,128]{1,0:T(8,128)} %fusion.132, f32[1024,128]{1,0:T(8,128)} %fusion.41, f32[512,1024]{1,0:T(8,128)} %copy-done.6, f32[1024]{0:T(1024)S(1)} %copy-done.84, f32[1024]{0:T(1024)S(1)} %get-tuple-element.43, f32[1024]{0:T(1024)S(1)} %get-tuple-element.44, ...), kind=kOutput, calls=%fused_computation.105 | convolution fusion | flops 136445952 | bytes 3551232 | tf_op jit(solution)/shard_map/dot_general | solution.py:39
  222.6 2.1 fusion.4
  227.0 2.5 fusion.53
  229.5 1.8 reshape.485
  231.3 2.1 fusion.6
  235.6 2.3 fusion.52
  237.9 1.8 reshape.487
  239.7 2.1 fusion.8
  244.1 2.3 fusion.51
  246.4 1.8 reshape.489
  248.2 2.1 fusion.10
  252.6 2.3 fusion.50
  254.9 1.8 reshape.491
  256.7 2.1 fusion.12
  261.1 2.3 fusion.49
  263.4 1.8 reshape.493
  267.6 1.6 fusion.48
  270.0 2.0 fusion
  273.4 2.3 fusion.55
  277.6 1.8 select_convert_fusion
  (282 shorter events, 48.9 us)
Async XLA Ops:
  6.5 69.4 %reduce-scatter.3.cloned.1.call-start = ((), (), s32[]{:S(2)}) async-start(), calls=%async_computation.2 | async-start | bytes 2228224 | tf_op jit(solution)/shard_map/reduce_scatter | solution.py:85
  11.2 129.2 %reduce-scatter.5.cloned.1.call-start = ((), (), s32[]{:S(2)}) async-start(), calls=%async_computation.4 | async-start | bytes 2228224 | tf_op jit(solution)/shard_map/reduce_scatter | solution.py:86
  12.0 167.4 %all-gather.3.cloned.1.call-start = ((), (), s32[]{:S(2)}) async-start(), calls=%async_computation.3 | async-start | bytes 1114112 | tf_op jit(solution)/shard_map/all_gather | solution.py:89
  14.7 27.2 %copy-start.52 = (bf16[128,1024]{1,0:T(8,128)(2,1)S(1)}, bf16[128,1024]{1,0:T(8,128)(2,1)}, u32[]{:S(2)}) copy-start(bf16[128,1024]{1,0:T(8,128)(2,1)} %param.10) | copy-start | bytes 786436
  14.8 32.4 %copy-start.20 = (bf16[1024,128]{1,0:T(8,128)(2,1)}, bf16[1024,128]{1,0:T(8,128)(2,1)S(1)}, u32[]{:S(2)}) copy-start(bf16[1024,128]{1,0:T(8,128)(2,1)S(1)} %reshape.484) | copy-start | bytes 786436
  15.1 28.1 %copy-start.27 = (bf16[1024,128]{1,0:T(8,128)(2,1)}, bf16[1024,128]{1,0:T(8,128)(2,1)S(1)}, u32[]{:S(2)}) copy-start(bf16[1024,128]{1,0:T(8,128)(2,1)S(1)} %reshape.494) | copy-start | bytes 786436
  15.4 29.4 %copy-start.24 = (bf16[1024,128]{1,0:T(8,128)(2,1)}, bf16[1024,128]{1,0:T(8,128)(2,1)S(1)}, u32[]{:S(2)}) copy-start(bf16[1024,128]{1,0:T(8,128)(2,1)S(1)} %reshape.492) | copy-start | bytes 786436
  42.9 146.0 %copy-start.70 = (f32[1024]{0:T(1024)}, f32[1024]{0:T(1024)S(1)}, u32[]{:S(2)}) copy-start(f32[1024]{0:T(1024)S(1)} %get-tuple-element.95) | copy-start | bytes 12292
  43.2 137.8 %copy-start.68 = (f32[1024]{0:T(1024)}, f32[1024]{0:T(1024)S(1)}, u32[]{:S(2)}) copy-start(f32[1024]{0:T(1024)S(1)} %get-tuple-element.89) | copy-start | bytes 12292
  43.2 56.2 %copy-start.38 = (bf16[128,1024]{1,0:T(8,128)(2,1)S(1)}, bf16[128,1024]{1,0:T(8,128)(2,1)}, u32[]{:S(2)}) copy-start(bf16[128,1024]{1,0:T(8,128)(2,1)} %get-tuple-element.53) | copy-start | bytes 786436
  44.8 54.7 %copy-start.37 = (bf16[128,1024]{1,0:T(8,128)(2,1)S(1)}, bf16[128,1024]{1,0:T(8,128)(2,1)}, u32[]{:S(2)}) copy-start(bf16[128,1024]{1,0:T(8,128)(2,1)} %get-tuple-element.54) | copy-start | bytes 786436
  44.8 54.8 %copy-start.36 = (bf16[128,1024]{1,0:T(8,128)(2,1)S(1)}, bf16[128,1024]{1,0:T(8,128)(2,1)}, u32[]{:S(2)}) copy-start(bf16[128,1024]{1,0:T(8,128)(2,1)} %get-tuple-element.55) | copy-start | bytes 786436
  45.7 54.1 %copy-start.35 = (bf16[128,1024]{1,0:T(8,128)(2,1)S(1)}, bf16[128,1024]{1,0:T(8,128)(2,1)}, u32[]{:S(2)}) copy-start(bf16[128,1024]{1,0:T(8,128)(2,1)} %get-tuple-element.56) | copy-start | bytes 786436
  77.5 140.7 %all-gather.5.cloned.1.call-start = ((), (), s32[]{:S(2)}) async-start(), calls=%async_computation.5 | async-start | bytes 1114112 | tf_op jit(solution)/shard_map/all_gather | solution.py:90
  99.5 11.8 %copy-start.22 = (bf16[1024,128]{1,0:T(8,128)(2,1)}, bf16[1024,128]{1,0:T(8,128)(2,1)S(1)}, u32[]{:S(2)}) copy-start(bf16[1024,128]{1,0:T(8,128)(2,1)S(1)} %reshape.482) | copy-start | bytes 786436
  99.6 8.4 %copy-start.30 = (bf16[1024,128]{1,0:T(8,128)(2,1)}, bf16[1024,128]{1,0:T(8,128)(2,1)S(1)}, u32[]{:S(2)}) copy-start(bf16[1024,128]{1,0:T(8,128)(2,1)S(1)} %reshape.490) | copy-start | bytes 786436
  99.7 8.3 %copy-start.28 = (bf16[1024,128]{1,0:T(8,128)(2,1)}, bf16[1024,128]{1,0:T(8,128)(2,1)S(1)}, u32[]{:S(2)}) copy-start(bf16[1024,128]{1,0:T(8,128)(2,1)S(1)} %reshape.488) | copy-start | bytes 786436
  99.9 8.1 %copy-start.25 = (bf16[1024,128]{1,0:T(8,128)(2,1)}, bf16[1024,128]{1,0:T(8,128)(2,1)S(1)}, u32[]{:S(2)}) copy-start(bf16[1024,128]{1,0:T(8,128)(2,1)S(1)} %reshape.486) | copy-start | bytes 786436
  179.4 6.8 %copy-start.33 = (bf16[512,1024]{1,0:T(8,128)(2,1)S(1)}, bf16[512,1024]{1,0:T(8,128)(2,1)}, u32[]{:S(2)}) copy-start(bf16[512,1024]{1,0:T(8,128)(2,1)} %all-gather.3.cloned.1.call-done) | copy-start | bytes 3145732
  180.9 8.6 %copy-start.19 = (f32[1024,128]{0,1:T(8,128)S(1)}, f32[1024,128]{0,1:T(8,128)}, u32[]{:S(2)}) copy-start(f32[1024,128]{0,1:T(8,128)} %get-tuple-element.92) | copy-start | bytes 1572868
  182.3 24.9 %copy-start.56 = (f32[1024]{0:T(1024)}, f32[1024]{0:T(1024)S(1)}, u32[]{:S(2)}) copy-start(f32[1024]{0:T(1024)S(1)} %get-tuple-element.62) | copy-start | bytes 12292
  184.0 6.2 %copy-start.34 = (bf16[128,1024]{1,0:T(8,128)(2,1)S(1)}, bf16[128,1024]{1,0:T(8,128)(2,1)}, u32[]{:S(2)}) copy-start(bf16[128,1024]{1,0:T(8,128)(2,1)} %all_gather.15) | copy-start | bytes 786436
  186.2 5.1 %copy-start.31 = (bf16[1024,128]{1,0:T(8,128)(2,1)S(1)}, bf16[1024,128]{1,0:T(8,128)(2,1)}, u32[]{:S(2)}) copy-start(bf16[1024,128]{1,0:T(8,128)(2,1)} %copy-done.30) | copy-start | bytes 786436
  188.9 4.8 %copy-start.18 = (f32[1024,128]{0,1:T(8,128)S(1)}, f32[1024,128]{0,1:T(8,128)}, u32[]{:S(2)}) copy-start(f32[1024,128]{0,1:T(8,128)} %get-tuple-element.98) | copy-start | bytes 1572868
  189.6 17.6 %copy-start.58 = (f32[1024]{0:T(1024)}, f32[1024]{0:T(1024)S(1)}, u32[]{:S(2)}) copy-start(f32[1024]{0:T(1024)S(1)} %get-tuple-element.64) | copy-start | bytes 12292
  193.1 4.4 %copy-start.26 = (bf16[1024,128]{1,0:T(8,128)(2,1)S(1)}, bf16[1024,128]{1,0:T(8,128)(2,1)}, u32[]{:S(2)}) copy-start(bf16[1024,128]{1,0:T(8,128)(2,1)} %copy-done.25) | copy-start | bytes 786436
  193.7 13.5 %copy-start.62 = (f32[1024]{0:T(1024)}, f32[1024]{0:T(1024)S(1)}, u32[]{:S(2)}) copy-start(f32[1024]{0:T(1024)S(1)} %get-tuple-element.66) | copy-start | bytes 12292
  196.1 4.4 %copy-start.21 = (bf16[1024,128]{1,0:T(8,128)(2,1)S(1)}, bf16[1024,128]{1,0:T(8,128)(2,1)}, u32[]{:S(2)}) copy-start(bf16[1024,128]{1,0:T(8,128)(2,1)} %copy-done.20) | copy-start | bytes 786436
  196.8 10.4 %copy-start.63 = (f32[1024]{0:T(1024)}, f32[1024]{0:T(1024)S(1)}, u32[]{:S(2)}) copy-start(f32[1024]{0:T(1024)S(1)} %get-tuple-element.68) | copy-start | bytes 12292
  196.8 13.5 %copy-start.53 = (f32[1024]{0:T(1024)}, f32[1024]{0:T(1024)S(1)}, u32[]{:S(2)}) copy-start(f32[1024]{0:T(1024)S(1)} %get-tuple-element.31) | copy-start | bytes 12292
  199.3 4.4 %copy-start.23 = (bf16[1024,128]{1,0:T(8,128)(2,1)S(1)}, bf16[1024,128]{1,0:T(8,128)(2,1)}, u32[]{:S(2)}) copy-start(bf16[1024,128]{1,0:T(8,128)(2,1)} %copy-done.22) | copy-start | bytes 786436
  199.9 7.3 %copy-start.64 = (f32[1024]{0:T(1024)}, f32[1024]{0:T(1024)S(1)}, u32[]{:S(2)}) copy-start(f32[1024]{0:T(1024)S(1)} %get-tuple-element.70) | copy-start | bytes 12292
  199.9 11.4 %copy-start.54 = (f32[1024]{0:T(1024)}, f32[1024]{0:T(1024)S(1)}, u32[]{:S(2)}) copy-start(f32[1024]{0:T(1024)S(1)} %get-tuple-element.36) | copy-start | bytes 12292
  203.0 9.4 %copy-start.55 = (f32[1024]{0:T(1024)}, f32[1024]{0:T(1024)S(1)}, u32[]{:S(2)}) copy-start(f32[1024]{0:T(1024)S(1)} %get-tuple-element.41) | copy-start | bytes 12292
  204.2 4.9 %copy-start.83 = (f32[1024]{0:T(1024)}, f32[1024]{0:T(1024)S(1)}, u32[]{:S(2)}) copy-start(f32[1024]{0:T(1024)S(1)} %get-tuple-element.47) | copy-start | bytes 12292
  212.4 5.9 %copy-start.84 = (f32[1024]{0:T(1024)S(1)}, f32[1024]{0:T(1024)}, u32[]{:S(2)}) copy-start(f32[1024]{0:T(1024)} %copy-done.83) | copy-start | bytes 12292
  222.6 4.4 %copy-start.5 = (f32[512,1024]{1,0:T(8,128)S(1)}, f32[512,1024]{1,0:T(8,128)}, u32[]{:S(2)}) copy-start(f32[512,1024]{1,0:T(8,128)} %get-tuple-element.118) | copy-start | bytes 6291460
  222.6 4.4 %copy-start.51 = (f32[1024,128]{1,0:T(8,128)S(1)}, f32[1024,128]{1,0:T(8,128)}, u32[]{:S(2)}) copy-start(f32[1024,128]{1,0:T(8,128)} %fusion.130) | copy-start | bytes 1572868
  222.6 4.4 %copy-start.82 = (f32[1024]{0:T(1024)S(1)}, f32[1024]{0:T(1024)}, u32[]{:S(2)}) copy-start(f32[1024]{0:T(1024)} %get-tuple-element.42) | copy-start | bytes 12292
  231.3 4.4 %copy-start.80 = (f32[1024]{0:T(1024)S(1)}, f32[1024]{0:T(1024)}, u32[]{:S(2)}) copy-start(f32[1024]{0:T(1024)} %get-tuple-element.37) | copy-start | bytes 12292
  239.7 4.4 %copy-start.3 = (f32[512,1024]{1,0:T(8,128)S(1)}, f32[512,1024]{1,0:T(8,128)}, u32[]{:S(2)}) copy-start(f32[512,1024]{1,0:T(8,128)} %get-tuple-element.106) | copy-start | bytes 6291460
  239.7 4.4 %copy-start.49 = (f32[1024,128]{1,0:T(8,128)S(1)}, f32[1024,128]{1,0:T(8,128)}, u32[]{:S(2)}) copy-start(f32[1024,128]{1,0:T(8,128)} %fusion.126) | copy-start | bytes 1572868
  239.7 4.4 %copy-start.79 = (f32[1024]{0:T(1024)S(1)}, f32[1024]{0:T(1024)}, u32[]{:S(2)}) copy-start(f32[1024]{0:T(1024)} %get-tuple-element.32) | copy-start | bytes 12292
  248.2 4.4 %copy-start.78 = (f32[1024]{0:T(1024)S(1)}, f32[1024]{0:T(1024)}, u32[]{:S(2)}) copy-start(f32[1024]{0:T(1024)} %get-tuple-element.27) | copy-start | bytes 12292
  254.9 4.6 %copy-start.59 = (f32[1024]{0:T(1024)S(1)}, f32[1024]{0:T(1024)}, u32[]{:S(2)}) copy-start(f32[1024]{0:T(1024)} %copy-done.58) | copy-start | bytes 12292
  256.7 4.4 %copy-start = (f32[512,1024]{1,0:T(8,128)S(1)}, f32[512,1024]{1,0:T(8,128)}, u32[]{:S(2)}) copy-start(f32[512,1024]{1,0:T(8,128)} %get-tuple-element.94) | copy-start | bytes 6291460
  256.7 4.4 %copy-start.46 = (f32[1024,128]{1,0:T(8,128)S(1)}, f32[1024,128]{1,0:T(8,128)}, u32[]{:S(2)}) copy-start(f32[1024,128]{1,0:T(8,128)} %fusion.122) | copy-start | bytes 1572868
  256.7 4.4 %copy-start.73 = (f32[1024]{0:T(1024)S(1)}, f32[1024]{0:T(1024)}, u32[]{:S(2)}) copy-start(f32[1024]{0:T(1024)} %get-tuple-element.22) | copy-start | bytes 12292
  (56 other events, 150.4 us)
Sparse Core Ops, SparseCore 0:
  11.4 64.5 reduce-scatter.2
  79.7 60.6 reduce-scatter.4
  142.6 36.7 all-gather.2
  181.4 36.7 all-gather.4
where the time goes:
time: 287 us; the launch traced here: 286 us
  waiting for transfers between devices  93.3 us (33%)
  matrix products  76.8 us (27%)
  blocking collectives  45.6 us (16%)
  other arithmetic  38.8 us (14%)
  local copies, waits for them, and re-layouts  16.5 us (6%)
  between operations  14.9 us (5%)
    dot_general x24, matrix products, attend(): jnp.dot(weights.astype(jnp.bfloat16), head_values, preferred_element_type...  40.5 us
    all_gather x1, waiting for transfers between devices, body(): lax.all_gather(part_keys.astype(jnp.bfloat16), 'ctx', axis=0, tiled=True)  37.4 us
    dot_general x24, matrix products, attend(): lax.dot_general(head_queries[kv_head], head_keys, (((1,), (1,)), ((), ())...  36.3 us
    reduce_scatter x1, waiting for transfers between devices, body(): lax.psum_scatter(mine_values, 'ctx', scatter_dimension=0, tiled=True)  27.5 us
    reduce_scatter x1, waiting for transfers between devices, body(): lax.psum_scatter(mine_keys, 'ctx', scatter_dimension=0, tiled=True)  27 us
    all_gather x1, blocking collectives, body(): lax.all_gather(prefix_keys, 'ctx', axis=0, tiled=True)  23.8 us
    all_gather x1, blocking collectives, body(): lax.all_gather(prefix_values, 'ctx', axis=0, tiled=True)  21.8 us
    reduce_sum x16, other arithmetic, attend(): new_totals.append(totals[kv_head] * shrink + jnp.sum(weights, axis=1))  20.7 us
  transfers between devices with their start and end apart: 4, of which 4 were waited for; matrix products, arithmetic and copies ran while one was open for 23% of the time, Pallas kernels for 0%

commit v1 on v0

--- a/solution.py
+++ b/solution.py
@@ -90,9 +90,13 @@
         lax.all_gather(part_values.astype(jnp.bfloat16), "ctx", axis=0, tiled=True),
     )
     carried = attend(carried, head_queries, shared_keys, shared_values, None)
+    obtain_counts_here = lambda a0: jnp.concatenate(
+        lax.all_to_all(jnp.stack([a0] * lax.axis_size("ctx")), "ctx", split_axis=0, concat_axis=0),
+        0,
+    )
     whole_keys, whole_values = (
         lax.all_gather(prefix_keys, "ctx", axis=0, tiled=True),
-        lax.all_gather(prefix_values, "ctx", axis=0, tiled=True),
+        obtain_counts_here(prefix_values),
     )
     carried = attend(carried, head_queries, whole_keys, whole_values, None)
     maxima, totals, accums = carried

time: 287 us -> 294 us (1.024)
  blocking collectives: 45.6 us -> 22.5 us
  waiting for transfers between devices: 93.3 us -> 107 us
  starting transfers between devices: 0.12 us -> 7.77 us
  matrix products: 76.8 us -> 82.2 us
    all_gather x1 -> x0, blocking collectives: 21.8 us -> none  [body(): lax.all_gather(prefix_values, 'ctx', axis=0, tiled=True)]
    reduce_scatter x1, waiting for transfers between devices: 27.5 us -> 47.5 us  [body(): lax.psum_scatter(mine_values, 'ctx', scatter_dimension=0, tiled=True)]
    all_to_all x0 -> x1, starting transfers between devices: none -> 7.46 us  [body(): lax.all_to_all(jnp.stack([a0] * lax.axis_size('ctx')), 'ctx', split_axis=...]
    dot_general x24, matrix products: 40.5 us -> 45.9 us  [attend(): jnp.dot(weights.astype(jnp.bfloat16), head_values, preferred_element_type...]
    reduce_scatter x1, waiting for transfers between devices: 27 us -> 21.8 us  [body(): lax.psum_scatter(mine_keys, 'ctx', scatter_dimension=0, tiled=True)]
  transfers between devices with their start and end apart: 4 -> 5, of which waited for: 4 -> 3; matrix products, arithmetic and copies ran while one was open for 23% -> 24% of each run, Pallas kernels for 0% -> 0%
where the time goes in v1:
time: 294 us; the launch traced here: 292 us
  waiting for transfers between devices  107 us (36%)
  matrix products  82.2 us (28%)
  other arithmetic  38.8 us (13%)
  blocking collectives  22.5 us (8%)
  local copies, waits for them, and re-layouts  18.4 us (6%)
  between operations  14.9 us (5%)
  starting transfers between devices  7.77 us (3%)
    reduce_scatter x1, waiting for transfers between devices, body(): lax.psum_scatter(mine_values, 'ctx', scatter_dimension=0, tiled=True)  47.5 us
    dot_general x24, matrix products, attend(): jnp.dot(weights.astype(jnp.bfloat16), head_values, preferred_element_type...  45.9 us
    all_gather x1, waiting for transfers between devices, body(): lax.all_gather(part_keys.astype(jnp.bfloat16), 'ctx', axis=0, tiled=True)  37.4 us
    dot_general x24, matrix products, attend(): lax.dot_general(head_queries[kv_head], head_keys, (((1,), (1,)), ((), ())...  36.3 us
    all_gather x1, blocking collectives, body(): lax.all_gather(prefix_keys, 'ctx', axis=0, tiled=True)  22.5 us
    reduce_scatter x1, waiting for transfers between devices, body(): lax.psum_scatter(mine_keys, 'ctx', scatter_dimension=0, tiled=True)  21.8 us
    reduce_sum x16, other arithmetic, attend(): new_totals.append(totals[kv_head] * shrink + jnp.sum(weights, axis=1))  20.7 us
    reshape x8, local copies, waits for them, and re-layouts, body(): (accums[kv_head] / totals[kv_head][:, None]).reshape(rows_here, group_siz...  12.5 us
  transfers between devices with their start and end apart: 5, of which 3 were waited for; matrix products, arithmetic and copies ran while one was open for 24% of the time, Pallas kernels for 0%

profile of v1, /device:TPU:0, one launch (start us, length us, event | category | flops | bytes accessed | tf_op | source)
XLA Modules:
  0.0 291.9 jit_solution(1359053525430773678)
XLA Ops:
  7.3 3.9 %convert_select_fusion = (f32[512,1024]{1,0:T(8,128)}, f32[512,1024]{1,0:T(8,128)}) fusion(bf16[1,2,256,1024]{3,2,1,0:T(8,128)(2,1)} %param.15, pred[512]{0:T(512)(128)(4,1)S(1)} %broadcast_in_dim.53, bf16[1,2,256,1024]{3,2,1,0:T(8,128)(2,1)} %param.14), kind=kLoop, calls=%fused_computation.1 | loop fusion | flops 2097152 | bytes 6291968 | tf_op jit(solution)/shard_map/jit(_where)/select_n | solution.py:81
  12.7 7.5 %all-to-all-start = ((bf16[16,8,1024]{2,1,0:T(8,128)(2,1)}), bf16[16,8,1024]{2,1,0:T(8,128)(2,1)}, u32[]{:S(2)}, u32[]{:S(2)}) async-start(bf16[16,8,1024]{2,1,0:T(8,128)(2,1)} %stack.2), calls=%async_computation.2 | async-start | bytes 524288 | tf_op jit(solution)/shard_map/all_to_all | solution.py:94
  23.6 22.5 %all_gather.11 = bf16[128,1024]{1,0:T(8,128)(2,1)S(1)} all-gather(bf16[8,1024]{1,0:T(8,128)(2,1)S(1)} %copy-done.97), channel_id=1, replica_groups=mesh['groups'=2,'ctx'=16] {'ctx'}, dimensions={0}, use_global_device_ids=true | all-gather | bytes 278528 | tf_op jit(solution)/shard_map/all_gather | solution.py:98
  52.5 1.6 fusion.270
  54.1 21.8 %reduce-scatter.3.cloned.1.call-done = f32[32,1024]{1,0:T(8,128)} async-done(((f32[512,1024]{1,0:T(8,128)}), f32[32,1024]{1,0:T(8,128)}) %reduce-scatter.3.cloned.1.call-update) | async-done | bytes 131088 | tf_op jit(solution)/shard_map/reduce_scatter | solution.py:85
  77.7 1.6 fusion.271
  79.9 1.6 fusion.268
  81.6 1.6 fusion.269
  84.8 1.6 fusion.267
  91.3 1.6 fusion.273
  92.9 47.5 %reduce-scatter.5.cloned.1.call-done = f32[32,1024]{1,0:T(8,128)} async-done(((f32[512,1024]{1,0:T(8,128)}), f32[32,1024]{1,0:T(8,128)}) %reduce-scatter.5.cloned.1.call-update) | async-done | bytes 131088 | tf_op jit(solution)/shard_map/reduce_scatter | solution.py:86
  142.0 37.4 %all-gather.3.cloned.1.call-done = bf16[512,1024]{1,0:T(8,128)(2,1)} async-done(((bf16[32,1024]{1,0:T(8,128)(2,1)}), bf16[512,1024]{1,0:T(8,128)(2,1)}) %all-gather.3.cloned.1.call-update) | async-done | bytes 1048592 | tf_op jit(solution)/shard_map/all_gather | solution.py:89
  182.2 1.7 fusion.94
  183.9 2.2 fusion.120
  186.0 2.9 multiply_reduce_fusion.1
  190.2 1.9 fusion.122
  192.1 1.8 multiply_reduce_fusion.2
  195.2 1.8 multiply_reduce_fusion.3
  198.3 1.8 multiply_reduce_fusion.4
  201.4 1.8 multiply_reduce_fusion.5
  205.6 1.8 multiply_reduce_fusion.7
  210.0 1.8 fusion.124
  211.9 1.8 fusion.126
  213.7 1.8 fusion.128
  215.5 1.8 fusion.130
  217.4 1.8 fusion.132
  219.2 1.8 fusion.134
  221.0 2.0 fusion.41
  223.0 3.3 %fusion.54 = bf16[1024,128]{1,0:T(8,128)(2,1)} fusion(f32[1024,128]{1,0:T(8,128)} %fusion.132, f32[1024,128]{1,0:T(8,128)} %fusion.41, f32[512,1024]{1,0:T(8,128)} %copy-done.6, f32[1024]{0:T(1024)S(1)} %copy-done.83, f32[1024]{0:T(1024)S(1)} %get-tuple-element.43, f32[1024]{0:T(1024)S(1)} %get-tuple-element.44, ...), kind=kOutput, calls=%fused_computation.105 | convolution fusion | flops 136445952 | bytes 3551232 | tf_op jit(solution)/shard_map/dot_general | solution.py:39
  227.4 2.1 fusion.4
  231.8 2.5 fusion.53
  234.3 1.8 reshape.491
  236.1 2.1 fusion.6
  240.4 2.3 fusion.52
  242.7 1.8 reshape.493
  244.5 2.1 fusion.8
  248.9 2.3 fusion.51
  251.2 1.8 reshape.495
  252.9 2.1 fusion.10
  257.3 2.3 fusion.50
  259.6 1.8 reshape.497
  261.4 2.1 fusion.12
  265.8 2.3 fusion.49
  268.1 1.8 reshape.499
  274.8 2.0 fusion
  278.1 2.3 fusion.55
  280.5 1.8 reshape.487
  283.6 1.8 select_convert_fusion
  (284 shorter events, 53.8 us)
Async XLA Ops:
  6.5 69.4 %reduce-scatter.3.cloned.1.call-start = ((), (), s32[]{:S(2)}) async-start(), calls=%async_computation.3 | async-start | bytes 2228224 | tf_op jit(solution)/shard_map/reduce_scatter | solution.py:85
  11.2 10.5 %copy-start.32 = (bf16[128,8192]{1,0:T(8,128)(2,1)S(1)}, bf16[128,8192]{1,0:T(8,128)(2,1)}, u32[]{:S(2)}) copy-start(bf16[128,8192]{1,0:T(8,128)(2,1)} %param.9) | copy-start | bytes 6291460
  11.3 129.2 %reduce-scatter.5.cloned.1.call-start = ((), (), s32[]{:S(2)}) async-start(), calls=%async_computation.5 | async-start | bytes 2228224 | tf_op jit(solution)/shard_map/reduce_scatter | solution.py:86
  12.7 171.1 %all-to-all-start = ((bf16[16,8,1024]{2,1,0:T(8,128)(2,1)}), bf16[16,8,1024]{2,1,0:T(8,128)(2,1)}, u32[]{:S(2)}, u32[]{:S(2)}) async-start(bf16[16,8,1024]{2,1,0:T(8,128)(2,1)} %stack.2), calls=%async_computation.2 | async-start | bytes 524288 | tf_op jit(solution)/shard_map/all_to_all | solution.py:94
  20.2 159.2 %all-gather.3.cloned.1.call-start = ((), (), s32[]{:S(2)}) async-start(), calls=%async_computation.4 | async-start | bytes 1114112 | tf_op jit(solution)/shard_map/all_gather | solution.py:89
  22.9 25.8 %copy-start.51 = (bf16[128,1024]{1,0:T(8,128)(2,1)S(1)}, bf16[128,1024]{1,0:T(8,128)(2,1)}, u32[]{:S(2)}) copy-start(bf16[128,1024]{1,0:T(8,128)(2,1)} %param.10) | copy-start | bytes 786436
  23.0 54.7 %copy-start.20 = (bf16[1024,128]{1,0:T(8,128)(2,1)}, bf16[1024,128]{1,0:T(8,128)(2,1)S(1)}, u32[]{:S(2)}) copy-start(bf16[1024,128]{1,0:T(8,128)(2,1)S(1)} %reshape.490) | copy-start | bytes 786436
  23.3 26.7 %copy-start.27 = (bf16[1024,128]{1,0:T(8,128)(2,1)}, bf16[1024,128]{1,0:T(8,128)(2,1)S(1)}, u32[]{:S(2)}) copy-start(bf16[1024,128]{1,0:T(8,128)(2,1)S(1)} %reshape.500) | copy-start | bytes 786436
  23.6 26.4 %copy-start.24 = (bf16[1024,128]{1,0:T(8,128)(2,1)}, bf16[1024,128]{1,0:T(8,128)(2,1)S(1)}, u32[]{:S(2)}) copy-start(bf16[1024,128]{1,0:T(8,128)(2,1)S(1)} %reshape.498) | copy-start | bytes 786436
  49.7 139.2 %copy-start.69 = (f32[1024]{0:T(1024)}, f32[1024]{0:T(1024)S(1)}, u32[]{:S(2)}) copy-start(f32[1024]{0:T(1024)S(1)} %get-tuple-element.95) | copy-start | bytes 12292
  50.0 130.9 %copy-start.67 = (f32[1024]{0:T(1024)}, f32[1024]{0:T(1024)S(1)}, u32[]{:S(2)}) copy-start(f32[1024]{0:T(1024)S(1)} %get-tuple-element.89) | copy-start | bytes 12292
  50.0 29.4 %copy-start.37 = (bf16[128,1024]{1,0:T(8,128)(2,1)S(1)}, bf16[128,1024]{1,0:T(8,128)(2,1)}, u32[]{:S(2)}) copy-start(bf16[128,1024]{1,0:T(8,128)(2,1)} %get-tuple-element.53) | copy-start | bytes 786436
  50.0 29.5 %copy-start.36 = (bf16[128,1024]{1,0:T(8,128)(2,1)S(1)}, bf16[128,1024]{1,0:T(8,128)(2,1)}, u32[]{:S(2)}) copy-start(bf16[128,1024]{1,0:T(8,128)(2,1)} %get-tuple-element.54) | copy-start | bytes 786436
  51.6 28.0 %copy-start.35 = (bf16[128,1024]{1,0:T(8,128)(2,1)S(1)}, bf16[128,1024]{1,0:T(8,128)(2,1)}, u32[]{:S(2)}) copy-start(bf16[128,1024]{1,0:T(8,128)(2,1)} %get-tuple-element.55) | copy-start | bytes 786436
  51.6 28.2 %copy-start.34 = (bf16[128,1024]{1,0:T(8,128)(2,1)S(1)}, bf16[128,1024]{1,0:T(8,128)(2,1)}, u32[]{:S(2)}) copy-start(bf16[128,1024]{1,0:T(8,128)(2,1)} %get-tuple-element.56) | copy-start | bytes 786436
  77.5 145.5 %all-gather.5.cloned.1.call-start = ((), (), s32[]{:S(2)}) async-start(), calls=%async_computation.6 | async-start | bytes 1114112 | tf_op jit(solution)/shard_map/all_gather | solution.py:90
  79.5 11.8 %copy-start.22 = (bf16[1024,128]{1,0:T(8,128)(2,1)}, bf16[1024,128]{1,0:T(8,128)(2,1)S(1)}, u32[]{:S(2)}) copy-start(bf16[1024,128]{1,0:T(8,128)(2,1)S(1)} %reshape.488) | copy-start | bytes 786436
  79.6 8.4 %copy-start.30 = (bf16[1024,128]{1,0:T(8,128)(2,1)}, bf16[1024,128]{1,0:T(8,128)(2,1)S(1)}, u32[]{:S(2)}) copy-start(bf16[1024,128]{1,0:T(8,128)(2,1)S(1)} %reshape.496) | copy-start | bytes 786436
  79.8 8.3 %copy-start.28 = (bf16[1024,128]{1,0:T(8,128)(2,1)}, bf16[1024,128]{1,0:T(8,128)(2,1)S(1)}, u32[]{:S(2)}) copy-start(bf16[1024,128]{1,0:T(8,128)(2,1)S(1)} %reshape.494) | copy-start | bytes 786436
  79.9 8.1 %copy-start.25 = (bf16[1024,128]{1,0:T(8,128)(2,1)}, bf16[1024,128]{1,0:T(8,128)(2,1)S(1)}, u32[]{:S(2)}) copy-start(bf16[1024,128]{1,0:T(8,128)(2,1)S(1)} %reshape.492) | copy-start | bytes 786436
  183.9 5.7 %copy-start.19 = (f32[1024,128]{0,1:T(8,128)S(1)}, f32[1024,128]{0,1:T(8,128)}, u32[]{:S(2)}) copy-start(f32[1024,128]{0,1:T(8,128)} %get-tuple-element.92) | copy-start | bytes 1572868
  186.0 6.1 %copy-start.31 = (bf16[1024,128]{1,0:T(8,128)(2,1)S(1)}, bf16[1024,128]{1,0:T(8,128)(2,1)}, u32[]{:S(2)}) copy-start(bf16[1024,128]{1,0:T(8,128)(2,1)} %copy-done.30) | copy-start | bytes 786436
  186.0 6.1 %copy-start.33 = (bf16[512,1024]{1,0:T(8,128)(2,1)S(1)}, bf16[512,1024]{1,0:T(8,128)(2,1)}, u32[]{:S(2)}) copy-start(bf16[512,1024]{1,0:T(8,128)(2,1)} %all-gather.3.cloned.1.call-done) | copy-start | bytes 3145732
  188.9 4.9 %copy-start.71 = (f32[1024]{0:T(1024)S(1)}, f32[1024]{0:T(1024)}, u32[]{:S(2)}) copy-start(f32[1024]{0:T(1024)} %get-tuple-element.101) | copy-start | bytes 12292
  188.9 5.0 %copy-start.95 = (f32[1024]{0:T(1024)S(1)}, f32[1024]{0:T(1024)}, u32[]{:S(2)}) copy-start(f32[1024]{0:T(1024)} %get-tuple-element.97) | copy-start | bytes 12292
  188.9 5.6 %copy-start.18 = (f32[1024,128]{0,1:T(8,128)S(1)}, f32[1024,128]{0,1:T(8,128)}, u32[]{:S(2)}) copy-start(f32[1024,128]{0,1:T(8,128)} %get-tuple-element.98) | copy-start | bytes 1572868
  189.6 18.5 %copy-start.57 = (f32[1024]{0:T(1024)}, f32[1024]{0:T(1024)S(1)}, u32[]{:S(2)}) copy-start(f32[1024]{0:T(1024)S(1)} %get-tuple-element.64) | copy-start | bytes 12292
  190.2 5.0 %copy-start.29 = (bf16[1024,128]{1,0:T(8,128)(2,1)S(1)}, bf16[1024,128]{1,0:T(8,128)(2,1)}, u32[]{:S(2)}) copy-start(bf16[1024,128]{1,0:T(8,128)(2,1)} %copy-done.28) | copy-start | bytes 786436
  193.9 4.4 %copy-start.26 = (bf16[1024,128]{1,0:T(8,128)(2,1)S(1)}, bf16[1024,128]{1,0:T(8,128)(2,1)}, u32[]{:S(2)}) copy-start(bf16[1024,128]{1,0:T(8,128)(2,1)} %copy-done.25) | copy-start | bytes 786436
  194.5 13.5 %copy-start.61 = (f32[1024]{0:T(1024)}, f32[1024]{0:T(1024)S(1)}, u32[]{:S(2)}) copy-start(f32[1024]{0:T(1024)S(1)} %get-tuple-element.66) | copy-start | bytes 12292
  197.0 4.5 %copy-start.21 = (bf16[1024,128]{1,0:T(8,128)(2,1)S(1)}, bf16[1024,128]{1,0:T(8,128)(2,1)}, u32[]{:S(2)}) copy-start(bf16[1024,128]{1,0:T(8,128)(2,1)} %copy-done.20) | copy-start | bytes 786436
  197.6 10.4 %copy-start.62 = (f32[1024]{0:T(1024)}, f32[1024]{0:T(1024)S(1)}, u32[]{:S(2)}) copy-start(f32[1024]{0:T(1024)S(1)} %get-tuple-element.68) | copy-start | bytes 12292
  197.6 14.3 %copy-start.52 = (f32[1024]{0:T(1024)}, f32[1024]{0:T(1024)S(1)}, u32[]{:S(2)}) copy-start(f32[1024]{0:T(1024)S(1)} %get-tuple-element.31) | copy-start | bytes 12292
  200.1 4.4 %copy-start.23 = (bf16[1024,128]{1,0:T(8,128)(2,1)S(1)}, bf16[1024,128]{1,0:T(8,128)(2,1)}, u32[]{:S(2)}) copy-start(bf16[1024,128]{1,0:T(8,128)(2,1)} %copy-done.22) | copy-start | bytes 786436
  200.7 7.3 %copy-start.63 = (f32[1024]{0:T(1024)}, f32[1024]{0:T(1024)S(1)}, u32[]{:S(2)}) copy-start(f32[1024]{0:T(1024)S(1)} %get-tuple-element.70) | copy-start | bytes 12292
  200.7 12.9 %copy-start.53 = (f32[1024]{0:T(1024)}, f32[1024]{0:T(1024)S(1)}, u32[]{:S(2)}) copy-start(f32[1024]{0:T(1024)S(1)} %get-tuple-element.36) | copy-start | bytes 12292
  203.9 11.6 %copy-start.54 = (f32[1024]{0:T(1024)}, f32[1024]{0:T(1024)S(1)}, u32[]{:S(2)}) copy-start(f32[1024]{0:T(1024)S(1)} %get-tuple-element.41) | copy-start | bytes 12292
  205.0 4.9 %copy-start.82 = (f32[1024]{0:T(1024)}, f32[1024]{0:T(1024)S(1)}, u32[]{:S(2)}) copy-start(f32[1024]{0:T(1024)S(1)} %get-tuple-element.47) | copy-start | bytes 12292
  215.5 7.5 %copy-start.83 = (f32[1024]{0:T(1024)S(1)}, f32[1024]{0:T(1024)}, u32[]{:S(2)}) copy-start(f32[1024]{0:T(1024)} %copy-done.82) | copy-start | bytes 12292
  227.4 4.4 %copy-start.5 = (f32[512,1024]{1,0:T(8,128)S(1)}, f32[512,1024]{1,0:T(8,128)}, u32[]{:S(2)}) copy-start(f32[512,1024]{1,0:T(8,128)} %get-tuple-element.118) | copy-start | bytes 6291460
  227.4 4.4 %copy-start.50 = (f32[1024,128]{1,0:T(8,128)S(1)}, f32[1024,128]{1,0:T(8,128)}, u32[]{:S(2)}) copy-start(f32[1024,128]{1,0:T(8,128)} %fusion.130) | copy-start | bytes 1572868
  227.4 4.4 %copy-start.81 = (f32[1024]{0:T(1024)S(1)}, f32[1024]{0:T(1024)}, u32[]{:S(2)}) copy-start(f32[1024]{0:T(1024)} %get-tuple-element.42) | copy-start | bytes 12292
  244.5 4.4 %copy-start.78 = (f32[1024]{0:T(1024)S(1)}, f32[1024]{0:T(1024)}, u32[]{:S(2)}) copy-start(f32[1024]{0:T(1024)} %get-tuple-element.32) | copy-start | bytes 12292
  259.6 4.6 %copy-start.58 = (f32[1024]{0:T(1024)S(1)}, f32[1024]{0:T(1024)}, u32[]{:S(2)}) copy-start(f32[1024]{0:T(1024)} %copy-done.57) | copy-start | bytes 12292
  261.4 4.4 %copy-start = (f32[512,1024]{1,0:T(8,128)S(1)}, f32[512,1024]{1,0:T(8,128)}, u32[]{:S(2)}) copy-start(f32[512,1024]{1,0:T(8,128)} %get-tuple-element.94) | copy-start | bytes 6291460
  261.4 4.4 %copy-start.45 = (f32[1024,128]{1,0:T(8,128)S(1)}, f32[1024,128]{1,0:T(8,128)}, u32[]{:S(2)}) copy-start(f32[1024,128]{1,0:T(8,128)} %fusion.122) | copy-start | bytes 1572868
  261.4 4.4 %copy-start.72 = (f32[1024]{0:T(1024)S(1)}, f32[1024]{0:T(1024)}, u32[]{:S(2)}) copy-start(f32[1024]{0:T(1024)} %get-tuple-element.22) | copy-start | bytes 12292
  278.1 5.2 %copy-start.38 = (bf16[128,1024]{1,0:T(8,128)(2,1)S(1)}, bf16[128,1024]{1,0:T(8,128)(2,1)}, u32[]{:S(2)}) copy-start(bf16[128,1024]{1,0:T(8,128)(2,1)} %reshape.491) | copy-start | bytes 786436
  (57 other events, 158.8 us)
Sparse Core Ops, SparseCore 0:
  11.4 64.5 reduce-scatter.2
  79.7 60.6 reduce-scatter.4
  142.6 36.7 all-gather.2
  181.4 36.8 all-gather.4
